TPU v7x, 32 devices: a whole 2x2x4 slice. The times are simulated.
32 devices in a mesh: head: 4 (over x, core), seq: 8 (over z, y).
Axes of the slice: x: 2, y: 2, z: 4, core: 2. Of those that a mesh axis runs over, the one named last changes fastest.
Arguments:
- queries: bfloat16 [2048, 4096], P('seq', 'head'), may hold values from -160 to 160
- encodings: bfloat16 [24, 128, 1024], P('seq', None, 'head'), may hold values from -6 to 6
- kv_weight: bfloat16 [2, 1024, 4096], P(None, None, 'head'), may hold values from -0.1875 to 0.1875
- grad_out: bfloat16 [2048, 4096], P('seq', 'head'), may hold values from -6 to 6
- neighbour_owner: int32 [32, 2], replicated, may hold values from 0 to 7, all different within a row; in each aligned block of 4 rows (0 to 3, 4 to 7, ...) at most 2 rows name the same one
- neighbour_slot: int32 [32, 2], replicated, may hold values from 0 to 2
Outputs:
- attended: bfloat16 [2048, 4096], P('seq', 'head')
- query_grad: bfloat16 [32, 64, 4096], P('seq', 'head')
- encoding_grad: bfloat16 [24, 128, 1024], P('seq', None, 'head')
Inputs may be any that keep to these rules, and one draw needn't show every extreme that they name: `neighbour_owner`: the 2 owners of one span differ. Among the 4 spans of one index of seq (aligned blocks of rows), no owner is named more than 2 times, and in every draw some owner is named exactly 2 times.
All inputs are finite; a program needn't handle non-finite values.
Results may differ from a plain program's by a relative error of at most 0.019.
The roundings to bfloat16 on the way count: a program that leaves them out, or rounds other values in their place, can miss the bound.
Values may be sent and summed in bfloat16 or wider, within the bound.
A program may use at most 64 MiB of HBM per device.

v0:
```python
import jax
import jax.numpy as jnp
from jax import lax
from jax.sharding import PartitionSpec as P

HEAD_DIM = 128
SPAN = 64
NEIGHBOURS = 2
NEIGHBOUR_LEN = 128


def passed_along(array, axis, by):
    count = lax.axis_size(axis)
    pairs = [(i, i + by) for i in range(count) if 0 <= i + by < count]
    return lax.ppermute(array, axis, pairs)


def per_device(queries, encodings, kv_weight, grad_out, neighbour_owner, neighbour_slot):
    seq_count = lax.axis_size("seq")
    seq_index = lax.axis_index("seq")
    scale = HEAD_DIM ** (-0.5)
    token_rows = queries.shape[0]
    local_width = queries.shape[1]
    local_heads = local_width // HEAD_DIM
    spans_local = token_rows // SPAN
    groups = spans_local + 1
    requests = spans_local * NEIGHBOURS
    capacity = max(2, (requests + seq_count - 1) // seq_count)
    tile_rows = encodings.shape[0]
    slice_width = encodings.shape[2]
    window = NEIGHBOURS * NEIGHBOUR_LEN
    owners_all = neighbour_owner.reshape(seq_count, requests)
    slots_all = neighbour_slot.reshape(seq_count, requests)
    order = jnp.arange(requests)
    earlier = order[:, None] > order[None, :]
    same_owner = owners_all[:, :, None] == owners_all[:, None, :]
    ranks_all = jnp.sum((same_owner & earlier[None]).astype(jnp.int32), axis=2)
    my_owner = lax.dynamic_index_in_dim(owners_all, seq_index, 0, keepdims=False)
    my_rank = lax.dynamic_index_in_dim(ranks_all, seq_index, 0, keepdims=False)
    slot_place = my_owner * capacity + my_rank
    matched = (owners_all == seq_index)[:, :, None] & (
        ranks_all[:, :, None] == jnp.arange(capacity)[None, None, :]
    )
    matched = matched.astype(jnp.int32)
    chosen = jnp.sum(matched * slots_all[:, :, None], axis=1).reshape(-1)
    filled = jnp.sum(matched, axis=1).reshape(-1)
    target = jnp.where(filled > 0, chosen, tile_rows)
    outgoing = jnp.where(filled[:, None, None] > 0, encodings[chosen], jnp.zeros((), jnp.bfloat16))
    outgoing = outgoing.reshape(seq_count, capacity, NEIGHBOUR_LEN, slice_width)
    incoming = lax.all_to_all(outgoing, "seq", split_axis=0, concat_axis=0, tiled=True)
    picked = incoming.reshape(seq_count * capacity, NEIGHBOUR_LEN, slice_width)[slot_place]
    features = lax.all_gather(picked, "head", axis=2, tiled=True)
    projected = jnp.einsum(
        "rle,ced->crld", features, kv_weight, preferred_element_type=jnp.float32
    ).astype(jnp.bfloat16)
    by_span = projected.reshape(2, spans_local, window, local_width)
    carried = passed_along(by_span[:, -1], "seq", 1)
    extended = jnp.concatenate([carried[:, None], by_span], axis=1)
    extended = extended.reshape(2, groups, window, local_heads, HEAD_DIM)
    key_block = extended[0]
    value_block = extended[1]

    def padded_groups(rows):
        padded = jnp.concatenate(
            [
                jnp.zeros((1, local_width), rows.dtype),
                rows,
                jnp.zeros((SPAN - 1, local_width), rows.dtype),
            ],
            0,
        )
        return padded.reshape(groups, SPAN, local_heads, HEAD_DIM)

    query_pad = padded_groups(queries)
    grad_pad = padded_groups(grad_out)
    scores = (
        jnp.einsum("gqhd,gkhd->ghqk", query_pad, key_block, preferred_element_type=jnp.float32)
        * scale
    )
    top = jnp.max(scores, axis=-1, keepdims=True)
    expo = jnp.exp(scores - top)
    probs = expo / jnp.sum(expo, axis=-1, keepdims=True)
    probs_half = probs.astype(jnp.bfloat16)
    output = jnp.einsum(
        "ghqk,gkhd->gqhd", probs_half, value_block, preferred_element_type=jnp.float32
    )
    attended = output.reshape(groups * SPAN, local_width)[1 : 1 + token_rows].astype(jnp.bfloat16)
    dprob = jnp.einsum("gqhd,gkhd->ghqk", grad_pad, value_block, preferred_element_type=jnp.float32)
    delta = jnp.sum(probs * dprob, axis=-1, keepdims=True)
    dscore = (probs * (dprob - delta)).astype(jnp.bfloat16)
    qgrad = (
        jnp.einsum("ghqk,gkhd->gqhd", dscore, key_block, preferred_element_type=jnp.float32) * scale
    )
    kgrad = (
        jnp.einsum("ghqk,gqhd->gkhd", dscore, query_pad, preferred_element_type=jnp.float32) * scale
    )
    vgrad = jnp.einsum("ghqk,gqhd->gkhd", probs_half, grad_pad, preferred_element_type=jnp.float32)
    qgrad_rows = qgrad.reshape(groups * SPAN, local_width)[1 : 1 + token_rows].astype(jnp.bfloat16)
    qgrad_rows = qgrad_rows.reshape(spans_local, SPAN, local_width)
    query_grad = lax.all_to_all(qgrad_rows, "head", split_axis=1, concat_axis=2, tiled=True)
    kv_grad = jnp.stack([kgrad, vgrad], 0).reshape(2, groups, window, local_width)
    returned = passed_along(kv_grad[:, 0], "seq", -1)
    own_grad = kv_grad[:, 1:].at[:, -1].add(returned)
    grad_half = own_grad.astype(jnp.bfloat16).reshape(2, requests, NEIGHBOUR_LEN, local_width)
    flat_half = grad_half.reshape(2, requests * NEIGHBOUR_LEN, local_width)
    term = jnp.einsum("cnd,ced->ne", flat_half, kv_weight, preferred_element_type=jnp.float32)
    term = term.reshape(requests, NEIGHBOUR_LEN, -1)
    request_grad = lax.psum_scatter(term, "head", scatter_dimension=2, tiled=True)
    outgoing_grad = jnp.zeros((seq_count * capacity, NEIGHBOUR_LEN, slice_width), jnp.float32)
    outgoing_grad = outgoing_grad.at[slot_place].set(request_grad)
    outgoing_grad = outgoing_grad.reshape(seq_count, capacity, NEIGHBOUR_LEN, slice_width)
    incoming_grad = lax.all_to_all(outgoing_grad, "seq", split_axis=0, concat_axis=0, tiled=True)
    summed = jnp.zeros((tile_rows + 1, NEIGHBOUR_LEN, slice_width), jnp.float32)
    summed = summed.at[target].add(
        incoming_grad.reshape(seq_count * capacity, NEIGHBOUR_LEN, slice_width)
    )
    tile_grad = summed[:tile_rows]
    return (attended, query_grad, tile_grad.astype(jnp.bfloat16))


def solution(mesh):
    in_specs = (
        P("seq", "head"),
        P("seq", None, "head"),
        P(None, None, "head"),
        P("seq", "head"),
        P(),
        P(),
    )
    out_specs = (P("seq", "head"), P("seq", "head", None), P("seq", None, "head"))
    return jax.shard_map(
        per_device, mesh=mesh, in_specs=in_specs, out_specs=out_specs, check_vma=False
    )
```

profile of v0, /device:TPU:0, one launch (start us, length us, event | category | flops | bytes accessed | tf_op | source)
XLA Modules:
  0.0 320.8 jit_solution(1670462678393541136)
XLA Ops:
  7.2 0.8 copy.79
  8.4 0.8 copy.81
  9.8 0.6 gather_fusion
  10.4 1.1 broadcast_select_fusion
  11.5 7.3 %all-to-all-start = ((bf16[8,2,128,256]{3,2,1,0:T(8,128)(2,1)}), bf16[8,2,128,256]{3,2,1,0:T(8,128)(2,1)S(1)}, u32[]{:S(2)}, u32[]{:S(2)}) async-start(bf16[8,2,128,256]{3,2,1,0:T(8,128)(2,1)} %broadcast_select_fusion), calls=%async_computation | async-start | bytes 2097152 | tf_op jit(solution)/shard_map/all_to_all | solution.py:50
  18.9 25.7 %all-to-all-done = bf16[8,2,128,256]{3,2,1,0:T(8,128)(2,1)S(1)} async-done(((bf16[8,2,128,256]{3,2,1,0:T(8,128)(2,1)}), bf16[8,2,128,256]{3,2,1,0:T(8,128)(2,1)S(1)}, u32[]{:S(2)}, u32[]{:S(2)}) %all-to-all-start) | async-done | bytes 1048608 | tf_op jit(solution)/shard_map/all_to_all | solution.py:50
  44.5 1.4 gather_fusion.1
  46.0 22.0 %all-gather.3.cloned.1.call-done = bf16[8,128,1024]{2,1,0:T(8,128)(2,1)} async-done(((bf16[8,128,256]{2,1,0:T(8,128)(2,1)}), bf16[8,128,1024]{2,1,0:T(8,128)(2,1)}) %all-gather.3.cloned.1.call-update) | async-done | bytes 2097168 | tf_op jit(solution)/shard_map/all_gather | solution.py:52
  67.9 7.3 %convert_bitcast_fusion = bf16[2,8,128,1024]{3,2,0,1:T(8,128)(2,1)S(1)} fusion(bf16[2,1024,1024]{2,1,0:T(8,128)(2,1)} %param.10, bf16[8,128,1024]{2,1,0:T(8,128)(2,1)} %all-gather.3.cloned.1.call-done), kind=kOutput, calls=%fused_computation.16 | convolution fusion | flops 4297064448 | bytes 10485760 | tf_op jit(solution)/shard_map/rle,ced->crld/dot_general | solution.py:53
  75.3 0.6 copy.83
  76.0 3.6 %collective-permute-start = (bf16[2,256,1024]{2,1,0:T(8,128)(2,1)S(1)}, bf16[2,256,1024]{2,1,0:T(8,128)(2,1)S(1)}, u32[]{:S(2)}, u32[]{:S(2)}) collective-permute-start(bf16[2,256,1024]{2,1,0:T(8,128)(2,1)S(1)} %slice_bitcast_fusion), channel_id=1, source_target_pairs={{0,1},{1,2},{2,3},{3,4},{4,5},{5,6},{6,7},{8,9},{9,10},{10,11},{11... | collective-permute-start | bytes 3145736 | tf_op jit(solution)/shard_map/ppermute | solution.py:15
  79.7 0.6 maximum_bitcast_fusion.1
  80.3 1.0 copy.115
  81.4 20.8 %collective-permute-done = bf16[2,256,1024]{2,1,0:T(8,128)(2,1)S(1)} collective-permute-done((bf16[2,256,1024]{2,1,0:T(8,128)(2,1)S(1)}, bf16[2,256,1024]{2,1,0:T(8,128)(2,1)S(1)}, u32[]{:S(2)}, u32[]{:S(2)}) %collective-permute-start) | collective-permute-done | bytes 1048608 | tf_op jit(solution)/shard_map/ppermute | solution.py:15
  102.2 2.6 pad_maximum_fusion
  104.8 3.0 copy.86
  107.8 5.0 %copy.85 = bf16[1,5,256,1024]{2,3,1,0:T(8,128)(2,1)} copy(bf16[1,5,256,1024]{3,2,1,0:T(8,128)(2,1)} %get-tuple-element.18) | data formatting | bytes 5242880 | tf_op jit(solution)/shard_map/slice | solution.py:61
  112.7 0.5 fusion.32
  113.2 7.0 %fusion.49 = (f32[5,8,64]{2,1,0:T(8,128)S(1)}, f32[5,8,64,256]{3,2,1,0:T(8,128)S(1)}) fusion(f32[5,8,64,256]{3,2,1,0:T(8,128)S(1)} %fusion.32), kind=kOutput, calls=%fused_computation.77 | output fusion | flops 2621695 | bytes 5253120 | tf_op jit(solution)/shard_map/sub | solution.py:81
  120.2 10.1 %fusion.25 = f32[5,8,128,256]{3,2,1,0:T(8,128)} fusion(bf16[5,64,8,128]{3,2,1,0:T(8,128)(2,1)} %bitcast.121, f32[5,8,64]{2,1,0:T(8,128)S(1)} %get-tuple-element.23, f32[5,8,64,256]{3,2,1,0:T(8,128)} %copy-done.6), kind=kOutput, calls=%fused_computation.46 | convolution fusion | flops 171051776 | bytes 8529920 | tf_op jit(solution)/shard_map/ghqk,gqhd->gkhd/dot_general | solution.py:97
  130.3 6.0 %copy.102 = f32[1,5,256,1024]{3,2,0,1:T(8,128)} copy(f32[1,5,256,1024]{2,3,1,0:T(8,128)} %bitcast.108) | data formatting | bytes 10485760 | tf_op jit(solution)/shard_map/stack | solution.py:101
  136.3 3.0 multiply_reduce_fusion
  139.3 0.9 multiply_convert_fusion
  140.3 3.3 %broadcast_multiply_fusion = f32[5,8,128,256]{3,2,1,0:T(8,128)} fusion(bf16[5,8,64,256]{3,2,1,0:T(8,128)(2,1)S(1)} %multiply_convert_fusion, bf16[5,64,8,128]{3,2,1,0:T(8,128)(2,1)S(1)} %bitcast.107), kind=kOutput, calls=%fused_computation.19 | convolution fusion | flops 169082880 | bytes 7208960 | tf_op jit(solution)/shard_map/ghqk,gqhd->gkhd/dot_general | solution.py:95
  143.5 6.1 %copy.101 = f32[1,5,256,1024]{3,2,0,1:T(8,128)} copy(f32[1,5,256,1024]{2,3,1,0:T(8,128)} %bitcast.104) | data formatting | bytes 10485760 | tf_op jit(solution)/shard_map/stack | solution.py:101
  149.6 1.8 fusion.19
  151.5 1.8 collective-permute-start.1
  153.3 0.8 copy-done.2
  154.0 0.7 fusion.1
  154.8 0.4 copy.104
  155.2 46.3 %collective-permute-done.1 = f32[2,256,1024]{2,1,0:T(8,128)S(1)} collective-permute-done((f32[2,256,1024]{2,1,0:T(8,128)S(1)}, f32[2,256,1024]{2,1,0:T(8,128)S(1)}, u32[]{:S(2)}, u32[]{:S(2)}) %collective-permute-start.1) | collective-permute-done | bytes 2097184 | tf_op jit(solution)/shard_map/ppermute | solution.py:15
  201.8 6.1 %fusion.12 = f32[8,128,1024]{2,1,0:T(8,128)} fusion(bf16[8,128,2,1024]{3,1,0,2:T(8,128)(2,1)S(1)} %bitcast.109, bf16[2,1024,1024]{2,1,0:T(8,128)(2,1)S(1)} %copy-done.10), kind=kOutput, calls=%fused_computation.25 | convolution fusion | flops 4294967296 | bytes 12582912 | tf_op jit(solution)/shard_map/cnd,ced->ne/dot_general | solution.py:106
  207.9 1.7 copy-done.4
  209.6 2.3 fusion.23
  212.0 0.4 copy.94
  212.7 1.2 copy.95
  213.9 3.5 %all-to-all-start.1 = ((bf16[4,64,1024]{2,0,1:T(4,128)(2,1)}), bf16[4,64,1024]{2,0,1:T(4,128)(2,1)S(1)}, u32[]{:S(2)}, u32[]{:S(2)}) async-start(bf16[4,64,1024]{2,0,1:T(4,128)(2,1)} %copy.95), calls=%async_computation.1 | async-start | bytes 1048576 | tf_op jit(solution)/shard_map/all_to_all | solution.py:100
  217.4 35.4 %reduce-scatter.2.cloned.1.call-done = f32[8,128,256]{2,1,0:T(8,128)} async-done(((f32[8,128,1024]{2,1,0:T(8,128)}), f32[8,128,256]{2,1,0:T(8,128)}) %reduce-scatter.2.cloned.1.call-update) | async-done | bytes 1048592 | tf_op jit(solution)/shard_map/reduce_scatter | solution.py:108
  252.8 1.6 broadcast_in_dim.24
  254.3 2.9 scatter_fusion
  257.2 5.5 %all-to-all-start.2 = ((f32[8,2,128,256]{3,2,1,0:T(8,128)}), f32[8,2,128,256]{3,2,1,0:T(8,128)S(1)}, u32[]{:S(2)}, u32[]{:S(2)}) async-start(f32[8,2,128,256]{3,2,1,0:T(8,128)} %bitcast.32), calls=%async_computation.3 | async-start | bytes 4194304 | tf_op jit(solution)/shard_map/all_to_all | solution.py:112
  262.7 7.9 %fusion.24 = bf16[5,64,8,128]{3,1,2,0:T(8,128)(2,1)S(1)} fusion(bf16[5,256,8,128]{1,3,2,0:T(8,128)(2,1)} %bitcast.112, f32[5,8,64]{2,1,0:T(8,128)S(1)} %get-tuple-element.23, f32[5,8,64,256]{3,2,1,0:T(8,128)} %copy-done.6), kind=kOutput, calls=%fused_computation.39 | convolution fusion | flops 171379456 | bytes 5908480 | tf_op jit(solution)/shard_map/ghqk,gkhd->gqhd/dot_general | solution.py:84
  270.6 0.4 copy.90
  271.2 0.9 slice.73
  272.3 0.8 copy.112
  273.1 37.9 %all-to-all-done.2 = f32[8,2,128,256]{3,2,1,0:T(8,128)S(1)} async-done(((f32[8,2,128,256]{3,2,1,0:T(8,128)}), f32[8,2,128,256]{3,2,1,0:T(8,128)S(1)}, u32[]{:S(2)}, u32[]{:S(2)}) %all-to-all-start.2) | async-done | bytes 2097184 | tf_op jit(solution)/shard_map/all_to_all | solution.py:112
  311.0 2.2 scatter_fusion.1
  313.2 0.7 slice.106
  (56 shorter events, 2.3 us)
Async XLA Ops:
  7.2 2.6 copy-start
  11.5 33.0 %all-to-all-start = ((bf16[8,2,128,256]{3,2,1,0:T(8,128)(2,1)}), bf16[8,2,128,256]{3,2,1,0:T(8,128)(2,1)S(1)}, u32[]{:S(2)}, u32[]{:S(2)}) async-start(bf16[8,2,128,256]{3,2,1,0:T(8,128)(2,1)} %broadcast_select_fusion), calls=%async_computation | async-start | bytes 2097152 | tf_op jit(solution)/shard_map/all_to_all | solution.py:50
  18.8 49.2 %all-gather.3.cloned.1.call-start = ((), (), s32[]{:S(2)}) async-start(), calls=%async_computation.5 | async-start | bytes 2621440 | tf_op jit(solution)/shard_map/all_gather | solution.py:52
  45.9 206.8 %reduce-scatter.2.cloned.1.call-start = ((), (), s32[]{:S(2)}) async-start(), calls=%async_computation.4 | async-start | bytes 5242880 | tf_op jit(solution)/shard_map/reduce_scatter | solution.py:108
  75.3 4.4 %copy-start.8 = (bf16[256,1024]{1,0:T(8,128)(2,1)S(1)}, bf16[256,1024]{1,0:T(8,128)(2,1)}, u32[]{:S(2)}) copy-start(bf16[256,1024]{1,0:T(8,128)(2,1)} %param.11) | copy-start | bytes 1572868
  75.3 4.4 %copy-start.9 = (bf16[256,1024]{1,0:T(8,128)(2,1)S(1)}, bf16[256,1024]{1,0:T(8,128)(2,1)}, u32[]{:S(2)}) copy-start(bf16[256,1024]{1,0:T(8,128)(2,1)} %param.8) | copy-start | bytes 1572868
  76.0 26.2 %collective-permute-start = (bf16[2,256,1024]{2,1,0:T(8,128)(2,1)S(1)}, bf16[2,256,1024]{2,1,0:T(8,128)(2,1)S(1)}, u32[]{:S(2)}, u32[]{:S(2)}) collective-permute-start(bf16[2,256,1024]{2,1,0:T(8,128)(2,1)S(1)} %slice_bitcast_fusion), channel_id=1, source_target_pairs={{0,1},{1,2},{2,3},{3,4},{4,5},{5,6},{6,7},{8,9},{9,10},{10,11},{11... | collective-permute-start | bytes 3145736 | tf_op jit(solution)/shard_map/ppermute | solution.py:15
  107.8 5.0 %copy-start.3 = (bf16[1,5,256,1024]{2,3,1,0:T(8,128)(2,1)}, bf16[1,5,256,1024]{2,3,1,0:T(8,128)(2,1)S(1)}, u32[]{:S(2)}) copy-start(bf16[1,5,256,1024]{2,3,1,0:T(8,128)(2,1)S(1)} %copy.86) | copy-start | bytes 7864324
  113.2 7.0 %copy-start.6 = (f32[5,8,64,256]{3,2,1,0:T(8,128)}, f32[5,8,64,256]{3,2,1,0:T(8,128)S(1)}, u32[]{:S(2)}) copy-start(f32[5,8,64,256]{3,2,1,0:T(8,128)S(1)} %fusion.32) | copy-start | bytes 7864324
  140.3 3.3 %copy-start.5 = (bf16[5,8,64,256]{3,2,1,0:T(8,128)(2,1)}, bf16[5,8,64,256]{3,2,1,0:T(8,128)(2,1)S(1)}, u32[]{:S(2)}) copy-start(bf16[5,8,64,256]{3,2,1,0:T(8,128)(2,1)S(1)} %multiply_convert_fusion) | copy-start | bytes 3932164
  143.5 9.7 %slice-start = ((s8[5242880]{0:T(1024)(128)(4,1)}), s8[1048576]{0:T(1024)(128)(4,1)S(1)}, s32[]{:S(2)}) async-start(s8[5242880]{0:T(1024)(128)(4,1)} %bitcast.98), calls=%async_computation.6 | async-start | bytes 2097152
  149.6 3.6 %slice-start.1 = ((s8[5242880]{0:T(1024)(128)(4,1)}), s8[4194304]{0:T(1024)(128)(4,1)S(1)}, s32[]{:S(2)}) async-start(s8[5242880]{0:T(1024)(128)(4,1)} %bitcast.98), calls=%async_computation.7 | async-start | bytes 8388608
  149.6 4.4 %copy-start.2 = (f32[1,5,256,1024]{3,2,0,1:T(8,128)S(1)}, f32[1,5,256,1024]{3,2,0,1:T(8,128)}, u32[]{:S(2)}) copy-start(f32[1,5,256,1024]{3,2,0,1:T(8,128)} %copy.101) | copy-start | bytes 15728644
  151.5 50.0 %collective-permute-start.1 = (f32[2,256,1024]{2,1,0:T(8,128)S(1)}, f32[2,256,1024]{2,1,0:T(8,128)S(1)}, u32[]{:S(2)}, u32[]{:S(2)}) collective-permute-start(f32[2,256,1024]{2,1,0:T(8,128)S(1)} %fusion.19), channel_id=1, source_target_pairs={{1,0},{2,1},{3,2},{4,3},{5,4},{6,5},{7,6},{9,8},{10,9},{11,10},{12... | collective-permute-start | bytes 6291464 | tf_op jit(solution)/shard_map/ppermute | solution.py:15
  155.2 46.6 %copy-start.10 = (bf16[2,1024,1024]{2,1,0:T(8,128)(2,1)S(1)}, bf16[2,1024,1024]{2,1,0:T(8,128)(2,1)}, u32[]{:S(2)}) copy-start(bf16[2,1024,1024]{2,1,0:T(8,128)(2,1)} %param.10) | copy-start | bytes 12582916
  207.9 1.7 copy-start.4
  213.9 43.3 %all-to-all-start.1 = ((bf16[4,64,1024]{2,0,1:T(4,128)(2,1)}), bf16[4,64,1024]{2,0,1:T(4,128)(2,1)S(1)}, u32[]{:S(2)}, u32[]{:S(2)}) async-start(bf16[4,64,1024]{2,0,1:T(4,128)(2,1)} %copy.95), calls=%async_computation.1 | async-start | bytes 1048576 | tf_op jit(solution)/shard_map/all_to_all | solution.py:100
  252.8 1.6 copy-start.7
  257.2 53.8 %all-to-all-start.2 = ((f32[8,2,128,256]{3,2,1,0:T(8,128)}), f32[8,2,128,256]{3,2,1,0:T(8,128)S(1)}, u32[]{:S(2)}, u32[]{:S(2)}) async-start(f32[8,2,128,256]{3,2,1,0:T(8,128)} %bitcast.32), calls=%async_computation.3 | async-start | bytes 4194304 | tf_op jit(solution)/shard_map/all_to_all | solution.py:112
  311.0 2.9 copy-start.1
Sparse Core Ops, SparseCore 0:
  46.1 21.8 all-gather.2
  208.0 44.6 reduce-scatter.1
where the time goes:
time: 322 us; the launch traced here: 321 us
  waiting for transfers between devices  188 us (58%)
  matrix products  40.4 us (13%)
  local copies, waits for them, and re-layouts  38.5 us (12%)
  starting transfers between devices  21.8 us (7%)
  other arithmetic  17.8 us (6%)
  between operations  14.4 us (4%)
    ppermute x2, waiting for transfers between devices, passed_along(): return lax.ppermute(array, axis, pairs)  67 us
    all_to_all x1, waiting for transfers between devices, per_device(): lax.all_to_all(outgoing_grad, 'seq', split_axis=0, concat_axis=0, tiled=T...  37.9 us
    reduce_scatter x1, waiting for transfers between devices, per_device(): lax.psum_scatter(term, 'head', scatter_dimension=2, tiled=True)  35.4 us
    all_to_all x1, waiting for transfers between devices, per_device(): lax.all_to_all(outgoing, 'seq', split_axis=0, concat_axis=0, tiled=True)  25.7 us
    all_gather x1, waiting for transfers between devices, per_device(): features = lax.all_gather(picked, 'head', axis=2, tiled=True)  22 us
    another operation x2, local copies, waits for them, and re-layouts, per_device(): jnp.stack([kgrad, vgrad], 0).reshape(2, groups, window, local_width)  12.1 us
    dot_general x1, matrix products, per_device(): jnp.einsum('ghqk,gqhd->gkhd', probs_half, grad_pad, preferred_element_typ...  10.1 us
    dot_general x1, matrix products, per_device(): jnp.einsum('ghqk,gkhd->gqhd', probs_half, value_block, preferred_element_...  7.86 us
  transfers between devices with their start and end apart: 7, of which 6 were waited for; matrix products, arithmetic and copies ran while one was open for 7% of the time, Pallas kernels for 0%

commit v1 on v0

--- a/solution.py
+++ b/solution.py
@@ -7,6 +7,22 @@
 SPAN = 64
 NEIGHBOURS = 2
 NEIGHBOUR_LEN = 128
+
+
+def product_in_turn(value, axis, dim, term):
+    size, index, rows = (lax.axis_size(axis), lax.axis_index(axis), value.shape[dim])
+    right = [(i, (i + 1) % size) for i in range(size)]
+    behind = [(i, (i - 1) % size) for i in range(size)]
+    half = size // 2
+    from_left = from_right = value
+    subtotal = term(value, index * rows)
+    for step in range(1, half + 1):
+        from_left = lax.ppermute(from_left, axis, right)
+        if step < size - half:
+            from_right = lax.ppermute(from_right, axis, behind)
+            subtotal = subtotal + term(from_right, (index + step) % size * rows)
+        subtotal = subtotal + term(from_left, (index - step) % size * rows)
+    return subtotal
 
 
 def passed_along(array, axis, by):
@@ -49,9 +65,16 @@
     outgoing = outgoing.reshape(seq_count, capacity, NEIGHBOUR_LEN, slice_width)
     incoming = lax.all_to_all(outgoing, "seq", split_axis=0, concat_axis=0, tiled=True)
     picked = incoming.reshape(seq_count * capacity, NEIGHBOUR_LEN, slice_width)[slot_place]
-    features = lax.all_gather(picked, "head", axis=2, tiled=True)
-    projected = jnp.einsum(
-        "rle,ced->crld", features, kv_weight, preferred_element_type=jnp.float32
+    projected = product_in_turn(
+        picked,
+        "head",
+        2,
+        lambda part, at: jnp.einsum(
+            "rle,ced->crld",
+            part,
+            lax.dynamic_slice_in_dim(kv_weight, at, part.shape[2], axis=1),
+            preferred_element_type=jnp.float32,
+        ),
     ).astype(jnp.bfloat16)
     by_span = projected.reshape(2, spans_local, window, local_width)
     carried = passed_along(by_span[:, -1], "seq", 1)

time: 322 us -> 311 us (0.966)
  waiting for transfers between devices: 188 us -> 166 us
  matrix products: 40.4 us -> 51.8 us
    all_gather x1 -> x0, waiting for transfers between devices: 22 us -> none  [per_device(): features = lax.all_gather(picked, 'head', axis=2, tiled=True)]
    dot_general x1 -> x4, matrix products: 7.31 us -> 19.5 us  [per_device(): jnp.einsum('rle,ced->crld', part, lax.dynamic_slice_in_dim(kv_weight, at,...]
    ppermute x0 -> x3, waiting for transfers between devices: none -> 8.14 us  [the longest x2 8.14 us: product_in_turn(): from_left = lax.ppermute(from_left, axis, right)]
    slice x2 -> x1, local copies, waits for them, and re-layouts: 7.93 us -> 0.07 us  [per_device(): carried = passed_along(by_span[:, -1], 'seq', 1)]
    ppermute x2, waiting for transfers between devices: 67 us -> 59.7 us  [passed_along(): return lax.ppermute(array, axis, pairs)]
    reshape x0 -> x1, local copies, waits for them, and re-layouts: none -> 6.21 us  [per_device(): by_span = projected.reshape(2, spans_local, window, local_width)]
    sub x1, other arithmetic: 6.98 us -> 2.31 us  [per_device(): expo = jnp.exp(scores - top)]
    unnamed x32 -> x37, local copies, waits for them, and re-layouts: 5.43 us -> 9.72 us
  transfers between devices with their start and end apart: 7 -> 9, of which waited for: 6 -> 6; matrix products, arithmetic and copies ran while one was open for 7% -> 13% of each run, Pallas kernels for 0% -> 0%
where the time goes in v1:
time: 311 us; the launch traced here: 310 us
  waiting for transfers between devices  166 us (53%)
  matrix products  51.8 us (17%)
  local copies, waits for them, and re-layouts  39.6 us (13%)
  starting transfers between devices  23.6 us (8%)
  other arithmetic  15 us (5%)
  between operations  14.5 us (5%)
    ppermute x2, waiting for transfers between devices, passed_along(): return lax.ppermute(array, axis, pairs)  59.7 us
    all_to_all x1, waiting for transfers between devices, per_device(): lax.all_to_all(outgoing_grad, 'seq', split_axis=0, concat_axis=0, tiled=T...  37.9 us
    reduce_scatter x1, waiting for transfers between devices, per_device(): lax.psum_scatter(term, 'head', scatter_dimension=2, tiled=True)  34.1 us
    all_to_all x1, waiting for transfers between devices, per_device(): lax.all_to_all(outgoing, 'seq', split_axis=0, concat_axis=0, tiled=True)  25.7 us
    dot_general x4, matrix products, per_device(): jnp.einsum('rle,ced->crld', part, lax.dynamic_slice_in_dim(kv_weight, at,...  19.5 us
    another operation x2, local copies, waits for them, and re-layouts, per_device(): jnp.stack([kgrad, vgrad], 0).reshape(2, groups, window, local_width)  12.1 us
    unnamed x37, local copies, waits for them, and re-layouts  9.72 us
    dot_general x1, matrix products, per_device(): jnp.einsum('ghqk,gqhd->gkhd', probs_half, grad_pad, preferred_element_typ...  8.37 us
  transfers between devices with their start and end apart: 9, of which 6 were waited for; matrix products, arithmetic and copies ran while one was open for 13% of the time, Pallas kernels for 0%

profile of v1, /device:TPU:0, one launch (start us, length us, event | category | flops | bytes accessed | tf_op | source)
XLA Modules:
  0.0 309.9 jit_solution(15956934705859048028)
XLA Ops:
  7.2 0.8 copy.73
  8.4 0.8 copy.75
  9.8 0.6 gather_fusion
  10.4 1.1 broadcast_select_fusion
  11.5 7.3 %all-to-all-start = ((bf16[8,2,128,256]{3,2,1,0:T(8,128)(2,1)}), bf16[8,2,128,256]{3,2,1,0:T(8,128)(2,1)S(1)}, u32[]{:S(2)}, u32[]{:S(2)}) async-start(bf16[8,2,128,256]{3,2,1,0:T(8,128)(2,1)} %broadcast_select_fusion), calls=%async_computation | async-start | bytes 2097152 | tf_op jit(solution)/shard_map/all_to_all | solution.py:66
  18.9 25.7 %all-to-all-done = bf16[8,2,128,256]{3,2,1,0:T(8,128)(2,1)S(1)} async-done(((bf16[8,2,128,256]{3,2,1,0:T(8,128)(2,1)}), bf16[8,2,128,256]{3,2,1,0:T(8,128)(2,1)S(1)}, u32[]{:S(2)}, u32[]{:S(2)}) %all-to-all-start) | async-done | bytes 1048608 | tf_op jit(solution)/shard_map/all_to_all | solution.py:66
  45.3 1.7 collective-permute-start
  46.9 2.5 fusion.25
  49.4 8.1 %collective-permute-done.1 = bf16[8,128,256]{2,1,0:T(8,128)(2,1)S(1)} collective-permute-done((bf16[8,128,256]{2,1,0:T(8,128)(2,1)S(1)}, bf16[8,128,256]{2,1,0:T(8,128)(2,1)S(1)}, u32[]{:S(2)}, u32[]{:S(2)}) %collective-permute-start.1) | collective-permute-done | bytes 524320 | tf_op jit(solution)/shard_map/ppermute | solution.py:20
  57.7 4.5 %fusion.21 = f32[2,1024,8,128]{1,3,2,0:T(8,128)} fusion(bf16[2,1024,1024]{2,1,0:T(8,128)(2,1)S(1)} %copy-done.9, s32[]{:T(128)S(6)} %select_n.87, bf16[8,128,256]{2,1,0:T(8,128)(2,1)S(1)} %collective-permute-done.1), kind=kOutput, calls=%fused_computation.38 | convolution fusion | flops 1073741824 | bytes 9961476 | tf_op jit(solution)/shard_map/rle,ced->crld/dot_general | solution.py:72
  62.2 4.5 %fusion.23 = f32[2,1024,8,128]{1,3,2,0:T(8,128)} fusion(bf16[2,1024,1024]{2,1,0:T(8,128)(2,1)S(1)} %copy-done.9, s32[]{:T(128)S(6)} %select_n.85, bf16[8,128,256]{2,1,0:T(8,128)(2,1)S(1)} %collective-permute-done), kind=kOutput, calls=%fused_computation.40 | convolution fusion | flops 1073741824 | bytes 9961476 | tf_op jit(solution)/shard_map/rle,ced->crld/dot_general | solution.py:72
  66.7 8.0 %add_convert_fusion = bf16[2,1024,8,128]{1,3,2,0:T(8,128)(2,1)S(1)} fusion(f32[2,1024,8,128]{1,3,2,0:T(8,128)} %fusion.21, f32[2,1024,8,128]{1,3,2,0:T(8,128)S(1)} %fusion.25, f32[2,1024,8,128]{1,3,2,0:T(8,128)} %fusion.23, bf16[2,1024,1024]{2,1,0:T(8,128)(2,1)} %param.10, s32[]{:T(128)S(6)} %select_n.89, bf16[8,128,256]{2,1,0:T(8,128)(2,1)S(1)} %collective-permute-done.2), kind=kOutput, calls=%fused_computation.10 | convolution fusion | flops 1082130432 | bytes 30932996 | tf_op jit(solution)/shard_map/rle,ced->crld/dot_general | solution.py:72
  74.8 1.9 copy-done.5
  76.8 1.3 copy.106
  78.1 3.6 %collective-permute-start.3 = (bf16[2,256,1024]{1,2,0:T(8,128)(2,1)}, bf16[2,256,1024]{1,2,0:T(8,128)(2,1)S(1)}, u32[]{:S(2)}, u32[]{:S(2)}) collective-permute-start(bf16[2,256,1024]{1,2,0:T(8,128)(2,1)} %bitcast.140), channel_id=1, source_target_pairs={{0,1},{1,2},{2,3},{3,4},{4,5},{5,6},{6,7},{8,9},{9,10},{10,11},{11... | collective-permute-start | bytes 3145736 | tf_op jit(solution)/shard_map/ppermute | solution.py:31
  81.8 1.7 maximum_bitcast_fusion.1
  83.6 1.0 copy.110
  84.5 6.2 %copy.78 = bf16[2,4,256,1024]{2,3,1,0:T(8,128)(2,1)} copy(bf16[2,4,256,1024]{3,2,1,0:T(8,128)(2,1)} %bitcast.122) | data formatting | bytes 8388608 | tf_op jit(solution)/shard_map/reshape | solution.py:79
  90.8 13.0 %collective-permute-done.3 = bf16[2,256,1024]{1,2,0:T(8,128)(2,1)S(1)} collective-permute-done((bf16[2,256,1024]{1,2,0:T(8,128)(2,1)}, bf16[2,256,1024]{1,2,0:T(8,128)(2,1)S(1)}, u32[]{:S(2)}, u32[]{:S(2)}) %collective-permute-start.3) | collective-permute-done | bytes 1048608 | tf_op jit(solution)/shard_map/ppermute | solution.py:31
  103.7 3.5 %pad_maximum_fusion = (bf16[1,5,256,1024]{2,3,1,0:T(8,128)(2,1)S(1)}, bf16[1,5,256,1024]{2,3,1,0:T(8,128)(2,1)}) fusion(bf16[2,4,256,1024]{2,3,1,0:T(8,128)(2,1)} %copy.78, bf16[2,1,256,1024]{2,3,1,0:T(8,128)(2,1)S(1)} %bitcast.139), kind=kLoop, calls=%fused_computation.16 | loop fusion | flops 2621440 | bytes 10485760 | tf_op jit(solution)/shard_map/concatenate | solution.py:81
  107.7 1.0 copy-done.3
  108.7 2.3 fusion.63
  111.0 8.4 %fusion.31 = f32[5,8,128,256]{3,2,1,0:T(8,128)} fusion(bf16[5,64,8,128]{3,2,1,0:T(8,128)(2,1)} %bitcast.141, f32[5,8,64]{2,1,0:T(8,128)S(1)} %get-tuple-element.23, f32[5,8,64,256]{3,2,1,0:T(8,128)S(1)} %fusion.38), kind=kOutput, calls=%fused_computation.53 | convolution fusion | flops 171051776 | bytes 8529920 | tf_op jit(solution)/shard_map/ghqk,gqhd->gkhd/dot_general | solution.py:120
  119.4 3.9 %multiply_reduce_fusion = (f32[5,8,64]{2,1,0:T(8,128)S(1)}, f32[5,8,64,256]{3,2,1,0:T(8,128)S(1)}) fusion(f32[5,8,64,256]{3,2,1,0:T(8,128)} %get-tuple-element.24, f32[5,8,64]{2,1,0:T(8,128)S(1)} %get-tuple-element.23, bf16[5,256,8,128]{1,3,2,0:T(8,128)(2,1)} %bitcast.130, bf16[5,64,8,128]{3,2,1,0:T(8,128)(2,1)} %bitcast.142), kind=kOutput, calls=%fused_computation.19 | convolution fusion | flops 169735680 | bytes 8540160 | tf_op jit(solution)/shard_map/gqhd,gkhd->ghqk/dot_general | solution.py:111
  123.3 0.9 multiply_convert_fusion
  124.2 3.3 %broadcast_multiply_fusion = f32[5,8,128,256]{3,2,1,0:T(8,128)} fusion(bf16[5,8,64,256]{3,2,1,0:T(8,128)(2,1)S(1)} %multiply_convert_fusion, bf16[5,64,8,128]{3,2,1,0:T(8,128)(2,1)S(1)} %bitcast.126), kind=kOutput, calls=%fused_computation.17 | convolution fusion | flops 169082880 | bytes 7208960 | tf_op jit(solution)/shard_map/ghqk,gqhd->gkhd/dot_general | solution.py:118
  127.5 6.0 %copy.93 = f32[1,5,256,1024]{3,2,0,1:T(8,128)} copy(f32[1,5,256,1024]{2,3,1,0:T(8,128)} %bitcast.123) | data formatting | bytes 10485760 | tf_op jit(solution)/shard_map/stack | solution.py:124
  133.5 6.1 %copy.94 = f32[1,5,256,1024]{3,2,0,1:T(8,128)} copy(f32[1,5,256,1024]{2,3,1,0:T(8,128)} %bitcast.127) | data formatting | bytes 10485760 | tf_op jit(solution)/shard_map/stack | solution.py:124
  139.6 1.8 fusion.15
  141.4 1.8 collective-permute-start.4
  143.2 0.8 copy-done.2
  144.0 0.7 fusion.1
  145.2 46.7 %collective-permute-done.4 = f32[2,256,1024]{2,1,0:T(8,128)S(1)} collective-permute-done((f32[2,256,1024]{2,1,0:T(8,128)S(1)}, f32[2,256,1024]{2,1,0:T(8,128)S(1)}, u32[]{:S(2)}, u32[]{:S(2)}) %collective-permute-start.4) | collective-permute-done | bytes 2097184 | tf_op jit(solution)/shard_map/ppermute | solution.py:31
  192.2 6.1 %fusion.8 = f32[8,128,1024]{2,1,0:T(8,128)} fusion(bf16[8,128,2,1024]{3,1,0,2:T(8,128)(2,1)S(1)} %bitcast.128, bf16[2,1024,1024]{2,1,0:T(8,128)(2,1)S(1)} %copy-done.10), kind=kOutput, calls=%fused_computation.23 | convolution fusion | flops 4294967296 | bytes 12582912 | tf_op jit(solution)/shard_map/cnd,ced->ne/dot_general | solution.py:129
  198.4 1.7 copy-done.4
  200.1 2.3 fusion.18
  203.1 1.2 copy.87
  204.3 3.5 %all-to-all-start.1 = ((bf16[4,64,1024]{2,0,1:T(4,128)(2,1)}), bf16[4,64,1024]{2,0,1:T(4,128)(2,1)S(1)}, u32[]{:S(2)}, u32[]{:S(2)}) async-start(bf16[4,64,1024]{2,0,1:T(4,128)(2,1)} %copy.87), calls=%async_computation.1 | async-start | bytes 1048576 | tf_op jit(solution)/shard_map/all_to_all | solution.py:123
  207.9 34.1 %reduce-scatter.2.cloned.1.call-done = f32[8,128,256]{2,1,0:T(8,128)} async-done(((f32[8,128,1024]{2,1,0:T(8,128)}), f32[8,128,256]{2,1,0:T(8,128)}) %reduce-scatter.2.cloned.1.call-update) | async-done | bytes 1048592 | tf_op jit(solution)/shard_map/reduce_scatter | solution.py:131
  242.0 1.6 broadcast_in_dim.24
  243.5 2.9 scatter_fusion
  246.4 5.5 %all-to-all-start.2 = ((f32[8,2,128,256]{3,2,1,0:T(8,128)}), f32[8,2,128,256]{3,2,1,0:T(8,128)S(1)}, u32[]{:S(2)}, u32[]{:S(2)}) async-start(f32[8,2,128,256]{3,2,1,0:T(8,128)} %bitcast.43), calls=%async_computation.3 | async-start | bytes 4194304 | tf_op jit(solution)/shard_map/all_to_all | solution.py:135
  251.9 7.9 %fusion.19 = bf16[5,64,8,128]{3,1,2,0:T(8,128)(2,1)S(1)} fusion(bf16[5,256,8,128]{1,3,2,0:T(8,128)(2,1)} %bitcast.131, f32[5,8,64]{2,1,0:T(8,128)S(1)} %get-tuple-element.23, f32[5,8,64,256]{3,2,1,0:T(8,128)} %copy-done.7), kind=kOutput, calls=%fused_computation.36 | convolution fusion | flops 171379456 | bytes 5908480 | tf_op jit(solution)/shard_map/ghqk,gkhd->gqhd/dot_general | solution.py:107
  260.4 0.9 slice.73
  261.4 0.8 copy.107
  262.3 37.9 %all-to-all-done.2 = f32[8,2,128,256]{3,2,1,0:T(8,128)S(1)} async-done(((f32[8,2,128,256]{3,2,1,0:T(8,128)}), f32[8,2,128,256]{3,2,1,0:T(8,128)S(1)}, u32[]{:S(2)}, u32[]{:S(2)}) %all-to-all-start.2) | async-done | bytes 2097184 | tf_op jit(solution)/shard_map/all_to_all | solution.py:135
  300.2 2.2 scatter_fusion.1
  302.4 0.7 slice.105
  (65 shorter events, 4.9 us)
Async XLA Ops:
  7.2 2.6 copy-start
  11.5 33.0 %all-to-all-start = ((bf16[8,2,128,256]{3,2,1,0:T(8,128)(2,1)}), bf16[8,2,128,256]{3,2,1,0:T(8,128)(2,1)S(1)}, u32[]{:S(2)}, u32[]{:S(2)}) async-start(bf16[8,2,128,256]{3,2,1,0:T(8,128)(2,1)} %broadcast_select_fusion), calls=%async_computation | async-start | bytes 2097152 | tf_op jit(solution)/shard_map/all_to_all | solution.py:66
  18.8 223.2 %reduce-scatter.2.cloned.1.call-start = ((), (), s32[]{:S(2)}) async-start(), calls=%async_computation.4 | async-start | bytes 5242880 | tf_op jit(solution)/shard_map/reduce_scatter | solution.py:131
  45.1 12.4 %collective-permute-start.1 = (bf16[8,128,256]{2,1,0:T(8,128)(2,1)S(1)}, bf16[8,128,256]{2,1,0:T(8,128)(2,1)S(1)}, u32[]{:S(2)}, u32[]{:S(2)}) collective-permute-start(bf16[8,128,256]{2,1,0:T(8,128)(2,1)S(1)} %gather_fusion.1), channel_id=1, source_target_pairs={{0,8},{8,16},{16,24},{24,0},{1,9},{9,17},{17,25},{25,1},{2,10},{10... | collective-permute-start | bytes 1572872 | tf_op jit(solution)/shard_map/ppermute | solution.py:20
  45.3 12.5 %copy-start.9 = (bf16[2,1024,1024]{2,1,0:T(8,128)(2,1)S(1)}, bf16[2,1024,1024]{2,1,0:T(8,128)(2,1)}, u32[]{:S(2)}) copy-start(bf16[2,1024,1024]{2,1,0:T(8,128)(2,1)} %param.10) | copy-start | bytes 12582916
  45.3 17.0 %collective-permute-start = (bf16[8,128,256]{2,1,0:T(8,128)(2,1)S(1)}, bf16[8,128,256]{2,1,0:T(8,128)(2,1)S(1)}, u32[]{:S(2)}, u32[]{:S(2)}) collective-permute-start(bf16[8,128,256]{2,1,0:T(8,128)(2,1)S(1)} %gather_fusion.1), channel_id=1, source_target_pairs={{0,24},{8,0},{16,8},{24,16},{1,25},{9,1},{17,9},{25,17},{2,26},{10... | collective-permute-start | bytes 1572872 | tf_op jit(solution)/shard_map/ppermute | solution.py:22
  57.6 9.2 %collective-permute-start.2 = (bf16[8,128,256]{2,1,0:T(8,128)(2,1)S(1)}, bf16[8,128,256]{2,1,0:T(8,128)(2,1)S(1)}, u32[]{:S(2)}, u32[]{:S(2)}) collective-permute-start(bf16[8,128,256]{2,1,0:T(8,128)(2,1)S(1)} %collective-permute-done.1), channel_id=1, source_target_pairs={{0,8},{8,16},{16,24},{24,0},{1,9},{9,17},{17,25},{25,1},{2,10},{10... | collective-permute-start | bytes 1572872 | tf_op jit(solution)/shard_map/ppermute | solution.py:20
  74.8 1.9 copy-start.5
  74.8 7.0 %copy-start.12 = (bf16[256,1024]{1,0:T(8,128)(2,1)S(1)}, bf16[256,1024]{1,0:T(8,128)(2,1)}, u32[]{:S(2)}) copy-start(bf16[256,1024]{1,0:T(8,128)(2,1)} %param.11) | copy-start | bytes 1572868
  78.1 25.6 %collective-permute-start.3 = (bf16[2,256,1024]{1,2,0:T(8,128)(2,1)}, bf16[2,256,1024]{1,2,0:T(8,128)(2,1)S(1)}, u32[]{:S(2)}, u32[]{:S(2)}) collective-permute-start(bf16[2,256,1024]{1,2,0:T(8,128)(2,1)} %bitcast.140), channel_id=1, source_target_pairs={{0,1},{1,2},{2,3},{3,4},{4,5},{5,6},{6,7},{8,9},{9,10},{10,11},{11... | collective-permute-start | bytes 3145736 | tf_op jit(solution)/shard_map/ppermute | solution.py:31
  107.2 1.5 copy-start.3
  108.7 2.3 copy-start.7
  119.4 3.9 %copy-start.8 = (f32[5,8,64,256]{3,2,1,0:T(8,128)S(1)}, f32[5,8,64,256]{3,2,1,0:T(8,128)}, u32[]{:S(2)}) copy-start(f32[5,8,64,256]{3,2,1,0:T(8,128)} %get-tuple-element.24) | copy-start | bytes 7864324
  124.2 3.3 %copy-start.6 = (bf16[5,8,64,256]{3,2,1,0:T(8,128)(2,1)}, bf16[5,8,64,256]{3,2,1,0:T(8,128)(2,1)S(1)}, u32[]{:S(2)}) copy-start(bf16[5,8,64,256]{3,2,1,0:T(8,128)(2,1)S(1)} %multiply_convert_fusion) | copy-start | bytes 3932164
  133.5 9.7 %slice-start = ((s8[5242880]{0:T(1024)(128)(4,1)}), s8[1048576]{0:T(1024)(128)(4,1)S(1)}, s32[]{:S(2)}) async-start(s8[5242880]{0:T(1024)(128)(4,1)} %bitcast.117), calls=%async_computation.5 | async-start | bytes 2097152
  139.6 3.6 %slice-start.1 = ((s8[5242880]{0:T(1024)(128)(4,1)}), s8[4194304]{0:T(1024)(128)(4,1)S(1)}, s32[]{:S(2)}) async-start(s8[5242880]{0:T(1024)(128)(4,1)} %bitcast.117), calls=%async_computation.6 | async-start | bytes 8388608
  139.6 4.4 %copy-start.2 = (f32[1,5,256,1024]{3,2,0,1:T(8,128)S(1)}, f32[1,5,256,1024]{3,2,0,1:T(8,128)}, u32[]{:S(2)}) copy-start(f32[1,5,256,1024]{3,2,0,1:T(8,128)} %copy.94) | copy-start | bytes 15728644
  141.4 50.5 %collective-permute-start.4 = (f32[2,256,1024]{2,1,0:T(8,128)S(1)}, f32[2,256,1024]{2,1,0:T(8,128)S(1)}, u32[]{:S(2)}, u32[]{:S(2)}) collective-permute-start(f32[2,256,1024]{2,1,0:T(8,128)S(1)} %fusion.15), channel_id=1, source_target_pairs={{1,0},{2,1},{3,2},{4,3},{5,4},{6,5},{7,6},{9,8},{10,9},{11,10},{12... | collective-permute-start | bytes 6291464 | tf_op jit(solution)/shard_map/ppermute | solution.py:31
  145.2 47.0 %copy-start.10 = (bf16[2,1024,1024]{2,1,0:T(8,128)(2,1)S(1)}, bf16[2,1024,1024]{2,1,0:T(8,128)(2,1)}, u32[]{:S(2)}) copy-start(bf16[2,1024,1024]{2,1,0:T(8,128)(2,1)} %param.10) | copy-start | bytes 12582916
  198.3 1.7 copy-start.4
  204.3 42.1 %all-to-all-start.1 = ((bf16[4,64,1024]{2,0,1:T(4,128)(2,1)}), bf16[4,64,1024]{2,0,1:T(4,128)(2,1)S(1)}, u32[]{:S(2)}, u32[]{:S(2)}) async-start(bf16[4,64,1024]{2,0,1:T(4,128)(2,1)} %copy.87), calls=%async_computation.1 | async-start | bytes 1048576 | tf_op jit(solution)/shard_map/all_to_all | solution.py:123
  242.0 1.6 copy-start.11
  246.4 53.7 %all-to-all-start.2 = ((f32[8,2,128,256]{3,2,1,0:T(8,128)}), f32[8,2,128,256]{3,2,1,0:T(8,128)S(1)}, u32[]{:S(2)}, u32[]{:S(2)}) async-start(f32[8,2,128,256]{3,2,1,0:T(8,128)} %bitcast.43), calls=%async_computation.3 | async-start | bytes 4194304 | tf_op jit(solution)/shard_map/all_to_all | solution.py:135
  300.2 2.9 copy-start.1
Sparse Core Ops, SparseCore 0:
  198.5 43.4 reduce-scatter.1
